TPU v7x, 256 devices: a whole 4x4x8 slice. The times are simulated.
256 devices in a mesh: section: 8 (over x, core), seq: 32 (over z, y).
Axes of the slice: x: 4, y: 4, z: 8, core: 2. Of those that a mesh axis runs over, the one named last changes fastest.
Arguments:
- query: bfloat16 [8, 16384, 1024], P('section', 'seq'), may hold values from -6 to 6
- key: bfloat16 [8, 16384, 1024], P('section', 'seq'), may hold values from -6 to 6
- value: bfloat16 [8, 16384, 1024], P('section', 'seq'), may hold values from -6 to 6
- grad_sent: bfloat16 [8, 16384, 2048], P('section', 'seq'), may hold values from -6 to 6
- out_weight: bfloat16 [8, 1024, 2048], P('section'), may hold values from -0.125 to 0.125
- assign: int32 [8, 4, 16384], P('section', None, 'seq'), may hold values from 0 to 7, as said below
Outputs:
- grad_query: bfloat16 [8, 16384, 1024], P('section', 'seq')
- grad_key: bfloat16 [8, 16384, 1024], P('section', 'seq')
- grad_value: bfloat16 [8, 16384, 1024], P('section', 'seq')
Inputs may be any that keep to these rules, and one draw needn't show every extreme that they name: `assign`: for each section and routing head, every cluster holds exactly 2048 tokens. The 512 tokens of one device put 1, 3, 5 or 7 times 112 // 7 tokens into one cluster, so at most 112, and some device reaches 112 for every section and head.
All inputs are finite; a program needn't handle non-finite values.
Results may differ from a plain program's by a relative error of at most 0.0058.
Values may be sent and summed in bfloat16 or wider, within the bound.
A program may use at most 128 MiB of HBM per device.

v0:
```python
import functools

import jax
import jax.numpy as jnp
from jax import lax
from jax.experimental import pallas as pl
from jax.experimental.pallas import tpu as pltpu
from jax.sharding import PartitionSpec as P

MESH = pl.DeviceIdType.MESH
BF = jnp.bfloat16
F32 = jnp.float32
I32 = jnp.int32
HR = 4
HD = 128
FACTOR = HD ** (-0.5)
NT = (((1,), (1,)), ((), ()))


def remote(src, dst, send, recv, device):
    return pltpu.make_async_remote_copy(
        src_ref=src, dst_ref=dst, send_sem=send, recv_sem=recv, device_id=device, device_id_type=MESH
    )


def place():
    sec = lax.axis_index("section")
    me = lax.axis_index("seq")
    return sec, me, (sec // 2) * 2, sec % 2, me // 4, me % 4


def plane_barrier(outside):
    sec, me, base, core, z, y = place()
    barrier = pltpu.get_barrier_semaphore()
    mine = core * 32 + me

    def greet(step, carry):
        other = (mine + step) % 64
        pl.semaphore_signal(
            barrier, inc=1, device_id=(base + other // 32, other % 32), device_id_type=MESH
        )
        return carry

    lax.fori_loop(1, 64, greet, 0)
    if outside:
        pl.semaphore_signal(
            barrier, inc=1, device_id=((sec + 2 * core + 7) % 8, me), device_id_type=MESH
        )
    pl.semaphore_wait(barrier, 64 if outside else 63)


def forward_kernel(
    q, k, v, grad_hbm, weight_hbm, rank_row, tiles,
    comp, grad_heads, halo_k, halo_v, tab,
    grad_in, weight, dense, mid0, mid1, mid2, mid3, pick, spread, arr0, arr1, arr2, arr3, counts, table,
    send_count, recv_count, send_grad, recv_grad, weight_sem, send_one, recv_one, send_two, recv_two,
    send_halo, recv_halo, table_sem,
):
    sec, me, base, core, z, y = place()
    seat = y * 2 + core
    parity = z % 2
    mid = (mid0, mid1, mid2, mid3)
    arrived = (arr0, arr1, arr2, arr3)
    get_weight = pltpu.make_async_copy(weight_hbm, weight, weight_sem)
    get_weight.start()
    plane_barrier(True)

    def count_copy(n):
        plane = 2 * (n // 8) + core
        dest_section = base + n % 2
        dest = plane * 4 + (n % 8) // 2
        own = (dest_section == sec) & (dest == me)
        copy = remote(
            tiles.at[n // 8], counts.at[me], send_count.at[n], recv_count, (dest_section, dest)
        )
        return own, copy

    def send_counts(n, carry):
        own, copy = count_copy(n)

        @pl.when(own)
        def _():
            pltpu.make_async_copy(tiles.at[n // 8], counts.at[me], recv_count).start()

        @pl.when(jnp.logical_not(own))
        def _():
            copy.start()

        return carry

    lax.fori_loop(0, 32, send_counts, 0)
    grad_copy = remote(grad_hbm, grad_in, send_grad, recv_grad, ((sec + 7) % 8, me))
    grad_copy.start()
    after = (sec, (me + 1) % 32)
    halo_copies = [
        remote(src.at[:, pl.ds(512, 512)], dst, send_halo.at[n], recv_halo.at[n], after)
        for n, (src, dst) in enumerate(((k, halo_k), (v, halo_v)))
    ]

    def one_copy(t, h):
        return remote(
            dense.at[t, h], mid[t].at[z // 2], send_one.at[t, h], recv_one.at[t, z // 2],
            (base + parity, (2 * h + core) * 4 + y),
        )

    def start_one(t, h):
        own = (2 * h + core) == z

        @pl.when(own)
        def _():
            pltpu.make_async_copy(dense.at[t, h], mid[t].at[z // 2], recv_one.at[t, z // 2]).start()

        @pl.when(jnp.logical_not(own))
        def _():
            one_copy(t, h).start()

    rows = lax.broadcasted_iota(I32, (512, 512), 0)
    for h in range(HR):
        pick[h] = jnp.where(rows == rank_row[h : h + 1, :], 1.0, 0.0).astype(BF)
    for t, src in enumerate((k, v, q)):
        for h in range(HR):
            rowsh = jnp.dot(pick[h], src[:, h * HD : (h + 1) * HD], preferred_element_type=F32)
            dense[t, h] = rowsh.astype(BF).reshape(32, 16, HD)
            start_one(t, h)
        if t == 0:
            for copy in halo_copies:
                copy.start()

    pltpu.make_async_copy(counts, counts, recv_count).wait()
    tab[0:32, :] = counts[:, 1, :]
    tab[72:104, :] = counts[:, 2, :]
    unit = counts[:, 0, :].astype(F32)
    below = (
        lax.broadcasted_iota(I32, (32, 32), 0) >= lax.broadcasted_iota(I32, (32, 32), 1)
    ).astype(F32)
    ends = jnp.dot(below, unit, preferred_element_type=F32)
    lane = lax.broadcasted_iota(I32, (32, 128), 1)
    mine = lane == seat
    my_end = jnp.sum(jnp.where(mine, ends, 0.0), axis=1, keepdims=True)
    my_unit = jnp.sum(jnp.where(mine, unit, 0.0), axis=1, keepdims=True)
    tab[32:64, :] = jnp.broadcast_to(my_end - my_unit, (32, 128)).astype(I32)
    passed = jnp.broadcast_to(my_end, (32, 128)) <= lane.astype(F32)
    source = jnp.sum(jnp.where(passed, 1.0, 0.0), axis=0, keepdims=True).astype(I32)
    begin = jnp.sum(jnp.where(passed, my_unit, 0.0), axis=0, keepdims=True).astype(I32)
    inside = lax.broadcasted_iota(I32, (1, 128), 1) - begin
    sz = source >> 2
    address = ((source & 3) * 2 + (sz & 1)) * 28 + (sz >> 1) * 7 + inside
    tab[64:72, :] = jnp.broadcast_to(address, (8, 128))
    table_copy = pltpu.make_async_copy(tab, table, table_sem)
    table_copy.start()
    table_copy.wait()

    def two_copy(t, d):
        c = (seat + d) % 8
        return remote(
            spread.at[t, d], arrived[t].at[pl.ds(seat * 28, 28)], send_two.at[t, d],
            recv_two.at[t, seat], (base + c % 2, z * 4 + c // 2),
        )

    def second_stage(t):
        for slot in range(4):
            remote(
                mid[t].at[slot], mid[t].at[slot], send_one.at[t, 0], recv_one.at[t, slot], (sec, me)
            ).wait_recv()

        def expand(d):
            c = (seat + d) % 8
            for slot in range(4):
                first = table[(slot * 2 + core) * 4 + y, c]
                for r in range(7):
                    spread[t, d, slot * 7 + r] = mid[t][slot, jnp.clip(first + r, 0, 31)]

        def step(d, carry):
            expand(d)
            two_copy(t, d).start()
            return carry

        lax.fori_loop(1, 8, step, 0)
        expand(0)
        pltpu.make_async_copy(
            spread.at[t, 0], arrived[t].at[pl.ds(seat * 28, 28)], recv_two.at[t, seat]
        ).start()

    second_stage(0)
    grad_copy.wait_recv()
    get_weight.wait()

    def project(n, carry):
        part = lax.dot_general(
            grad_in[...], weight[pl.ds(pl.multiple_of(n * 256, 256), 256), :], NT,
            preferred_element_type=F32,
        ).astype(BF)
        grad_heads[2 * n] = part[:, :HD]
        grad_heads[2 * n + 1] = part[:, HD:]
        return carry

    lax.fori_loop(0, 4, project, 0)
    for h in range(HR):
        rowsh = jnp.dot(pick[h], grad_heads[h], preferred_element_type=F32)
        dense[3, h] = rowsh.astype(BF).reshape(32, 16, HD)
        start_one(3, h)
    second_stage(1)
    second_stage(2)
    second_stage(3)
    for t in range(4):
        def await_two(j, carry, t=t):
            region = arrived[t].at[pl.ds(j * 28, 28)]
            remote(region, region, send_two.at[t, 0], recv_two.at[t, j], (sec, me)).wait_recv()
            return carry

        lax.fori_loop(0, 8, await_two, 0)

        def gather(n, carry, t=t):
            for m in range(8):
                comp[t, n * 8 + m] = arrived[t][jnp.clip(table[64, n * 8 + m], 0, 223)]
            return carry

        lax.fori_loop(0, 16, gather, 0)
    for copy in halo_copies:
        copy.wait()
    grad_copy.wait_send()

    def drain_counts(n, carry):
        own, copy = count_copy(n)

        @pl.when(jnp.logical_not(own))
        def _():
            copy.wait_send()

        return carry

    lax.fori_loop(0, 32, drain_counts, 0)
    for t in range(4):
        for h in range(HR):
            @pl.when((2 * h + core) != z)
            def _(t=t, h=h):
                one_copy(t, h).wait_send()

        def drain_two(d, carry, t=t):
            two_copy(t, d).wait_send()
            return carry

        lax.fori_loop(1, 8, drain_two, 0)


def return_kernel(
    answer, carry_grad, table,
    back, carry_in,
    spread, arr0, arr1, arr2, dense,
    send_one, recv_one, send_two, recv_two, send_carry, recv_carry,
):
    sec, me, base, core, z, y = place()
    seat = y * 2 + core
    arrived = (arr0, arr1, arr2)
    plane_barrier(False)
    carry_copy = remote(carry_grad, carry_in, send_carry, recv_carry, (sec, (me + 31) % 32))

    def one_copy(t, d):
        j = (seat + d) % 8
        return remote(
            spread.at[t, d], arrived[t].at[pl.ds(seat * 28, 28)], send_one.at[t, d],
            recv_one.at[t, seat], (base + j % 2, z * 4 + j // 2),
        )

    def expand(t, d):
        j = (seat + d) % 8
        for slot in range(4):
            first = table[32 + (slot * 2 + j % 2) * 4 + j // 2, 0]
            for r in range(7):
                spread[t, d, slot * 7 + r] = answer[t, jnp.clip(first + r, 0, 127)]

    for t in range(3):
        def step(d, carry, t=t):
            expand(t, d)
            one_copy(t, d).start()
            return carry

        lax.fori_loop(1, 8, step, 0)
        expand(t, 0)
        pltpu.make_async_copy(
            spread.at[t, 0], arrived[t].at[pl.ds(seat * 28, 28)], recv_one.at[t, seat]
        ).start()

    carry_copy.start()

    def two_copy(t, slot):
        return remote(
            dense.at[t, slot], back.at[t, z // 2], send_two.at[t, slot], recv_two.at[t, z // 2],
            (base + z % 2, (slot * 2 + core) * 4 + y),
        )

    def own_slot(slot):
        return ((slot * 2 + core) == z) & (z % 2 == core)

    for t in range(3):
        def await_one(j, carry, t=t):
            region = arrived[t].at[pl.ds(j * 28, 28)]
            remote(region, region, send_one.at[t, 0], recv_one.at[t, j], (sec, me)).wait_recv()
            return carry

        lax.fori_loop(0, 8, await_one, 0)
        for slot in range(4):
            row = 72 + (slot * 2 + core) * 4 + y

            def gather(n, carry, t=t, slot=slot, row=row):
                for m in range(8):
                    dense[t, slot, n * 8 + m] = arrived[t][jnp.clip(table[row, n * 8 + m] + slot * 7, 0, 223)]
                return carry

            lax.fori_loop(0, 4, gather, 0)

            @pl.when(own_slot(slot))
            def _(t=t, slot=slot):
                pltpu.make_async_copy(
                    dense.at[t, slot], back.at[t, z // 2], recv_two.at[t, z // 2]
                ).start()

            @pl.when(jnp.logical_not(own_slot(slot)))
            def _(t=t, slot=slot):
                two_copy(t, slot).start()

    for t in range(3):
        for h in range(HR):
            remote(
                back.at[t, h], back.at[t, h], send_two.at[t, 0], recv_two.at[t, h], (sec, me)
            ).wait_recv()
    carry_copy.wait()
    for t in range(3):
        def drain(d, carry, t=t):
            one_copy(t, d).wait_send()
            return carry

        lax.fori_loop(1, 8, drain, 0)
        for slot in range(4):
            @pl.when(jnp.logical_not(own_slot(slot)))
            def _(t=t, slot=slot):
                two_copy(t, slot).wait_send()


def block_rows(ref, index, first, count):
    return ref[index, pl.ds(first, count), :]


def attend(score, dprob, q_blk, g_blk, key_of, value_of, flip_of, masks, add):
    count = len(masks)
    top = None
    for n in range(count):
        s = lax.dot_general(key_of(n), q_blk, NT, preferred_element_type=F32) * FACTOR
        if masks[n] is not None:
            s = jnp.where(masks[n], s, -1e30)
        score[n] = s
        high = jnp.max(s, axis=0, keepdims=True)
        top = high if top is None else jnp.maximum(top, high)
    total = jnp.zeros((1, 256), F32)
    cross = jnp.zeros((1, 256), F32)
    for n in range(count):
        e = jnp.exp(score[n] - top)
        dp = lax.dot_general(value_of(n), g_blk, NT, preferred_element_type=F32)
        score[n] = e
        dprob[n] = dp
        total = total + jnp.sum(e, axis=0, keepdims=True)
        cross = cross + jnp.sum(e * dp, axis=0, keepdims=True)
    inverse = 1.0 / total
    delta = cross * inverse
    flipped = jnp.zeros((HD, 256), F32)
    for n in range(count):
        prob = score[n] * inverse
        ds = (prob * (dprob[n] - delta)).astype(BF)
        add(n, jnp.dot(ds, q_blk, preferred_element_type=F32),
            jnp.dot(prob.astype(BF), g_blk, preferred_element_type=F32))
        flipped = flipped + jnp.dot(flip_of(n), ds, preferred_element_type=F32)
    return (jnp.transpose(flipped) * FACTOR).astype(BF)


def compute_kernel(
    comp, q, k, v, grad_heads, halo_k, halo_v,
    answer, local_q, local_k, local_v, carry_grad,
    score, dprob, flip, total_k, total_v,
):
    me = lax.axis_index("seq")
    low = lax.broadcasted_iota(I32, (256, 256), 0)
    col = lax.broadcasted_iota(I32, (256, 256), 1)
    total_k[...] = jnp.zeros_like(total_k)
    total_v[...] = jnp.zeros_like(total_v)
    for n in range(8):
        flip[n] = jnp.transpose(comp[0, n * 256 : (n + 1) * 256, :].astype(F32)).astype(BF)
    causal = low <= col
    for blk in range(7, -1, -1):
        rows = slice(blk * 256, (blk + 1) * 256)

        def add(n, dk, dv):
            total_k[n * 256 : (n + 1) * 256, :] += dk
            total_v[n * 256 : (n + 1) * 256, :] += dv

        answer[2, rows, :] = attend(
            score, dprob, comp[2, rows, :], comp[3, rows, :],
            lambda n: comp[0, n * 256 : (n + 1) * 256, :],
            lambda n: comp[1, n * 256 : (n + 1) * 256, :],
            lambda n: flip[n],
            [None] * blk + [causal], add,
        )
        answer[0, rows, :] = (total_k[rows, :] * FACTOR).astype(BF)
        answer[1, rows, :] = total_v[rows, :].astype(BF)
    first_ok = me > 0
    for h in range(4):
        cols = slice((h + 4) * HD, (h + 5) * HD)
        half = slice(h * HD, (h + 1) * HD)

        def key_rows(n, halo, own):
            return halo[n * 256 : (n + 1) * 256, half] if n < 2 else own[(n - 2) * 256 : (n - 1) * 256, cols]

        for n in range(4):
            flip[n] = jnp.transpose(key_rows(n, halo_k, k).astype(F32)).astype(BF)
        total_k[0:1024, :] = jnp.zeros((1024, HD), F32)
        total_v[0:1024, :] = jnp.zeros((1024, HD), F32)
        for blk in range(2):
            rows = slice(blk * 256, (blk + 1) * 256)
            masks = [low > col, None, low <= col]
            for n in range(3):
                if blk + n < 2:
                    live = jnp.broadcast_to(first_ok, (256, 256))
                    masks[n] = live if masks[n] is None else masks[n] & live

            def add(n, dk, dv, blk=blk):
                spot = slice((blk + n) * 256, (blk + n + 1) * 256)
                total_k[spot, :] += dk
                total_v[spot, :] += dv

            local_q[h, rows, :] = attend(
                score, dprob, q[rows, cols], grad_heads[4 + h, rows, :],
                lambda n: key_rows(blk + n, halo_k, k),
                lambda n: key_rows(blk + n, halo_v, v),
                lambda n: flip[blk + n],
                masks, add,
            )
        carry_grad[0, h] = (total_k[0:512, :] * FACTOR).astype(BF)
        carry_grad[1, h] = total_v[0:512, :].astype(BF)
        local_k[h] = total_k[512:1024, :] * FACTOR
        local_v[h] = total_v[512:1024, :]


def finish_kernel(back, carry_in, rank_col, local_q, local_k, local_v, out_q, out_k, out_v):
    keep = lax.axis_index("seq") < 31
    cols = lax.broadcasted_iota(I32, (512, 512), 1)
    for h in range(HR):
        place_rows = jnp.where(cols == rank_col[:, h : h + 1], 1.0, 0.0).astype(BF)
        span = slice(h * HD, (h + 1) * HD)
        for t, out in enumerate((out_k, out_v, out_q)):
            out[:, span] = jnp.dot(place_rows, back[t, h], preferred_element_type=F32).astype(BF)
        span = slice((h + 4) * HD, (h + 5) * HD)
        out_q[:, span] = local_q[h]
        for t, (out, local) in enumerate(((out_k, local_k), (out_v, local_v))):
            extra = jnp.where(keep, carry_in[t, h].astype(F32), 0.0)
            out[:, span] = (local[h] + extra).astype(BF)


VM = pl.BlockSpec(memory_space=pltpu.VMEM)
SM = pl.BlockSpec(memory_space=pltpu.SMEM)
HBM = pl.BlockSpec(memory_space=pl.ANY)
SDS = jax.ShapeDtypeStruct
DMA = pltpu.SemaphoreType.DMA


def plan(labels):
    members = (labels[:, :, None] == jnp.arange(8, dtype=I32)[None, None, :]).astype(BF)
    ids = jnp.arange(512, dtype=I32)
    lower = (ids[:, None] >= ids[None, :]).astype(BF)
    running = jnp.einsum("ts,hsc->htc", lower, members, preferred_element_type=F32)
    counts = running[:, -1, :].astype(I32)
    clusters = jnp.arange(8, dtype=I32)
    ends = jnp.sum(jnp.where(clusters[:, None] <= clusters[None, :], counts[:, :, None], 0), axis=1)
    starts = ends - counts
    offset = running - 1.0 + starts.astype(F32)[:, None, :]
    ranks = jnp.sum(jnp.where(members > 0, offset, 0.0), axis=2).astype(I32)
    units, unit_start, unit_end = counts // 16, starts // 16, ends // 16
    lanes = jnp.arange(128, dtype=I32)
    passed = unit_end[:, :, None] <= lanes[None, None, :]
    which = jnp.sum(passed.astype(I32), axis=1)
    begun = jnp.sum(jnp.where(passed, units[:, :, None], 0), axis=1)
    inverse = jnp.where(lanes < 32, which * 28 + lanes - begun, 0)
    wide = lambda x: jnp.pad(x, ((0, 0), (0, 120)))
    zero = jnp.zeros_like(inverse)
    tiles = jnp.stack([wide(units), wide(unit_start), inverse] + [zero] * 5, axis=1)
    return ranks, tiles


def body(query, key, value, grad_sent, out_weight, assign):
    ranks, tiles = plan(assign[0])
    rank_row = jnp.pad(ranks, ((0, 4), (0, 0)))
    rank_col = rank_row.T
    q, k, v = query[0], key[0], value[0]
    comp, grad_heads, halo_k, halo_v, tab = pl.pallas_call(
        forward_kernel,
        out_shape=(
            SDS((4, 128, 16, HD), BF), SDS((8, 512, HD), BF), SDS((512, 512), BF),
            SDS((512, 512), BF), SDS((104, 128), I32),
        ),
        in_specs=[VM, VM, VM, HBM, HBM, VM, VM],
        out_specs=(VM, VM, VM, VM, VM),
        scratch_shapes=[
            pltpu.VMEM((512, 2048), BF), pltpu.VMEM((1024, 2048), BF),
            pltpu.VMEM((4, 4, 32, 16, HD), BF), *[pltpu.VMEM((4, 32, 16, HD), BF)] * 4,
            pltpu.VMEM((4, 512, 512), BF), pltpu.VMEM((4, 8, 28, 16, HD), BF),
            *[pltpu.VMEM((224, 16, HD), BF)] * 4, pltpu.VMEM((32, 8, 128), I32),
            pltpu.SMEM((104, 128), I32),
            DMA((32,)), DMA, DMA, DMA, DMA, DMA((4, 4)), DMA((4, 4)), DMA((4, 8)), DMA((4, 8)),
            DMA((2,)), DMA((2,)), DMA,
        ],
        compiler_params=pltpu.CompilerParams(collective_id=0, has_side_effects=True),
        name="exchange_forward",
    )(q, k, v, grad_sent[0], out_weight[0], rank_row, tiles)
    answer, local_q, local_k, local_v, carry_grad = pl.pallas_call(
        compute_kernel,
        out_shape=(
            SDS((3, 2048, HD), BF), SDS((4, 512, HD), BF), SDS((4, 512, HD), F32),
            SDS((4, 512, HD), F32), SDS((2, 4, 512, HD), BF),
        ),
        in_specs=[VM] * 7,
        out_specs=(VM,) * 5,
        scratch_shapes=[
            pltpu.VMEM((8, 256, 256), F32), pltpu.VMEM((8, 256, 256), F32),
            pltpu.VMEM((8, HD, 256), BF), pltpu.VMEM((2048, HD), F32), pltpu.VMEM((2048, HD), F32),
        ],
        name="attention_backward",
    )(comp.reshape(4, 2048, HD), q, k, v, grad_heads, halo_k, halo_v)
    back, carry_in = pl.pallas_call(
        return_kernel,
        out_shape=(SDS((3, 4, 32, 16, HD), BF), SDS((2, 4, 512, HD), BF)),
        in_specs=[VM, VM, SM],
        out_specs=(VM, VM),
        scratch_shapes=[
            pltpu.VMEM((3, 8, 28, 16, HD), BF), *[pltpu.VMEM((224, 16, HD), BF)] * 3,
            pltpu.VMEM((3, 4, 32, 16, HD), BF),
            DMA((3, 8)), DMA((3, 8)), DMA((3, 4)), DMA((3, 4)), DMA, DMA,
        ],
        compiler_params=pltpu.CompilerParams(collective_id=1, has_side_effects=True),
        name="exchange_return",
    )(answer.reshape(3, 128, 16, HD), carry_grad, tab)
    outs = pl.pallas_call(
        finish_kernel,
        out_shape=(SDS((512, 1024), BF),) * 3,
        in_specs=[VM] * 6,
        out_specs=(VM,) * 3,
        name="finish",
    )(back.reshape(3, 4, 512, HD), carry_in, rank_col, local_q, local_k, local_v)
    return tuple(out[None] for out in outs)


def solution(mesh):
    return jax.shard_map(
        body,
        mesh=mesh,
        in_specs=(P("section", "seq", None),) * 4
        + (P("section", None, None), P("section", None, "seq")),
        out_specs=(P("section", "seq", None),) * 3,
        check_vma=False,
    )
```

profile of v0, /device:TPU:25, one launch (start us, length us, event | category | flops | bytes accessed | tf_op | source)
XLA Modules:
  0.0 224.9 jit_solution(7729367278171843288)
XLA Ops:
  0.7 0.9 convolution_bitcast_fusion
  1.6 0.2 fusion.4
  1.8 0.1 select_reduce_fusion.2
  2.0 0.1 convert_reduce_fusion
  2.1 0.6 stack.16.tiles
  2.7 0.1 copy.23
  2.8 0.2 convert_reduce_fusion.1
  3.0 0.8 select_reduce_fusion
  3.8 0.1 copy.24
  4.0 0.1 copy.27
  4.1 0.7 pad_bitcast_fusion.rank_col
  4.8 0.6 pad.11.clone.rank_row
  5.4 92.0 %exchange_forward.1 = (bf16[4,128,16,128]{3,2,1,0:T(8,128)(2,1)}, bf16[8,512,128]{2,1,0:T(8,128)(2,1)}, bf16[512,512]{1,0:T(8,128)(2,1)}, bf16[512,512]{1,0:T(8,128)(2,1)}, s32[104,128]{1,0:T(8,128)}) custom-call(bf16[512,1024]{1,0:T(8,128)(2,1)} %bitcast.26, bf16[512,1024]{1,0:T(8,128)(2,1)} %bitcast.28, bf16[512,1024]{1,0:T(8,128)(2,1)} %bitcast.30, ...), custom_call_target="tpu_custom_call" | custom-call | tf_op jit(solution)/shard_map/exchange_forward/pallas_call | solution.py:492
  97.5 21.4 %attention_backward.1 = (bf16[3,2048,128]{2,1,0:T(8,128)(2,1)}, bf16[4,512,128]{2,1,0:T(8,128)(2,1)}, f32[4,512,128]{2,1,0:T(8,128)}, f32[4,512,128]{2,1,0:T(8,128)}, bf16[2,4,512,128]{3,2,1,0:T(8,128)(2,1)}) custom-call(bf16[4,2048,128]{2,1,0:T(8,128)(2,1)} %bitcast.33, bf16[512,1024]{1,0:T(8,128)(2,1)} %bitcast.27, bf16[512,1024]{1,0:T(8,128)(2,1)} %bitcast.29, ...), custom_call_target="tpu_custom_call" | custom-call | tf_op jit(solution)/shard_map/attention_backward/pallas_call | solution.py:512
  118.9 99.7 %exchange_return.1 = (bf16[3,4,32,16,128]{4,3,2,1,0:T(8,128)(2,1)}, bf16[2,4,512,128]{3,2,1,0:T(8,128)(2,1)}) custom-call(bf16[3,128,16,128]{3,2,1,0:T(8,128)(2,1)} %bitcast.35, bf16[2,4,512,128]{3,2,1,0:T(8,128)(2,1)} %get-tuple-element.23.carry_grad, s32[104,128]{1,0:T(8,128)} %get-tuple-element.24.table), custom_call_target="tpu_custom_call" | custom-call | tf_op jit(solution)/shard_map/exchange_return/pallas_call | solution.py:526
  218.6 6.3 %finish.1 = (bf16[512,1024]{1,0:T(8,128)(2,1)}, bf16[512,1024]{1,0:T(8,128)(2,1)}, bf16[512,1024]{1,0:T(8,128)(2,1)}) custom-call(bf16[3,4,512,128]{3,2,1,0:T(8,128)(2,1)} %bitcast.36, bf16[2,4,512,128]{3,2,1,0:T(8,128)(2,1)} %get-tuple-element.26.carry_in, s32[512,8]{1,0:T(8,128)} %pad_bitcast_fusion.rank_col, ...), custom_call_target="tpu_custom_call" | custom-call | tf_op jit(solution)/shard_map/finish/pallas_call | solution.py:539
  (10 shorter events, 0.1 us)
where the time goes:
time: 225 us
  Pallas kernels  219 us (97%)
  local copies, waits for them, and re-layouts  2.35 us (1%)
    pallas_call x1, Pallas kernels, body(): pl.pallas_call(return_kernel, out_shape=(SDS((3, 4, 32, 16, HD), BF), SDS...  99.7 us
    pallas_call x1, Pallas kernels, body(): pl.pallas_call(forward_kernel, out_shape=(SDS((4, 128, 16, HD), BF), SDS(...  92 us
    pallas_call x1, Pallas kernels, body(): pl.pallas_call(compute_kernel, out_shape=(SDS((3, 2048, HD), BF), SDS((4,...  21.4 us
    pallas_call x1, Pallas kernels, body(): pl.pallas_call(finish_kernel, out_shape=(SDS((512, 1024), BF),) * 3, in_s...  6.34 us

commit v1 on v0

--- a/solution.py
+++ b/solution.py
@@ -51,10 +51,11 @@
 
 def forward_kernel(
     q, k, v, grad_hbm, weight_hbm, rank_row, tiles,
-    comp, grad_heads, halo_k, halo_v, tab,
+    comp, tab, local_q, local_k, local_v, carry_in,
+    halo_k, halo_v, grad_heads, carry_grad, score, dprob, flip, total_k, total_v,
     grad_in, weight, dense, mid0, mid1, mid2, mid3, pick, spread, arr0, arr1, arr2, arr3, counts, table,
     send_count, recv_count, send_grad, recv_grad, weight_sem, send_one, recv_one, send_two, recv_two,
-    send_halo, recv_halo, table_sem,
+    send_halo, recv_halo, table_sem, send_carry, recv_carry,
 ):
     sec, me, base, core, z, y = place()
     seat = y * 2 + core
@@ -95,6 +96,14 @@
     halo_copies = [
         remote(src.at[:, pl.ds(512, 512)], dst, send_halo.at[n], recv_halo.at[n], after)
         for n, (src, dst) in enumerate(((k, halo_k), (v, halo_v)))
+    ]
+
+    carry_copies = [
+        remote(
+            carry_grad.at[pl.ds(2 * n, 2)], carry_in.at[pl.ds(2 * n, 2)],
+            send_carry.at[n], recv_carry.at[n], (sec, (me + 31) % 32),
+        )
+        for n in range(2)
     ]
 
     def one_copy(t, h):
@@ -200,7 +209,55 @@
         dense[3, h] = rowsh.astype(BF).reshape(32, 16, HD)
         start_one(3, h)
     second_stage(1)
+    low = lax.broadcasted_iota(I32, (256, 256), 0)
+    col = lax.broadcasted_iota(I32, (256, 256), 1)
+    behind = jnp.broadcast_to(me > 0, (256, 256))
+
+    def local_head(h, carry):
+        cols = pl.ds(pl.multiple_of((h + 4) * HD, HD), HD)
+        half = pl.ds(pl.multiple_of(h * HD, HD), HD)
+
+        def key_rows(n, halo, own):
+            if n < 2:
+                return halo[n * 256 : (n + 1) * 256, half]
+            return own[(n - 2) * 256 : (n - 1) * 256, cols]
+
+        for n in range(4):
+            flip[n] = jnp.transpose(key_rows(n, halo_k, k).astype(F32)).astype(BF)
+        total_k[...] = jnp.zeros_like(total_k)
+        total_v[...] = jnp.zeros_like(total_v)
+        for blk in range(2):
+            rows = slice(blk * 256, (blk + 1) * 256)
+            masks = [low > col, None, low <= col]
+            for n in range(3):
+                if blk + n < 2:
+                    masks[n] = behind if masks[n] is None else masks[n] & behind
+
+            def add(n, dk, dv, blk=blk):
+                spot = slice((blk + n) * 256, (blk + n + 1) * 256)
+                total_k[spot, :] += dk
+                total_v[spot, :] += dv
+
+            local_q[h, rows, :] = attend(
+                score, dprob, q[rows, cols], grad_heads[4 + h, rows, :],
+                lambda n: key_rows(blk + n, halo_k, k),
+                lambda n: key_rows(blk + n, halo_v, v),
+                lambda n: flip[blk + n],
+                masks, add,
+            )
+        carry_grad[h, 0] = (total_k[0:512, :] * FACTOR).astype(BF)
+        carry_grad[h, 1] = total_v[0:512, :].astype(BF)
+        local_k[h] = total_k[512:1024, :] * FACTOR
+        local_v[h] = total_v[512:1024, :]
+        return carry
+
+    for copy in halo_copies:
+        copy.wait_recv()
+    lax.fori_loop(0, 2, local_head, 0)
+    carry_copies[0].start()
     second_stage(2)
+    lax.fori_loop(2, 4, local_head, 0)
+    carry_copies[1].start()
     second_stage(3)
     for t in range(4):
         def await_two(j, carry, t=t):
@@ -217,6 +274,8 @@
 
         lax.fori_loop(0, 16, gather, 0)
     for copy in halo_copies:
+        copy.wait_send()
+    for copy in carry_copies:
         copy.wait()
     grad_copy.wait_send()
 
@@ -244,16 +303,15 @@
 
 
 def return_kernel(
-    answer, carry_grad, table,
-    back, carry_in,
+    answer, table,
+    back,
     spread, arr0, arr1, arr2, dense,
-    send_one, recv_one, send_two, recv_two, send_carry, recv_carry,
+    send_one, recv_one, send_two, recv_two,
 ):
     sec, me, base, core, z, y = place()
     seat = y * 2 + core
     arrived = (arr0, arr1, arr2)
     plane_barrier(False)
-    carry_copy = remote(carry_grad, carry_in, send_carry, recv_carry, (sec, (me + 31) % 32))
 
     def one_copy(t, d):
         j = (seat + d) % 8
@@ -281,8 +339,6 @@
             spread.at[t, 0], arrived[t].at[pl.ds(seat * 28, 28)], recv_one.at[t, seat]
         ).start()
 
-    carry_copy.start()
-
     def two_copy(t, slot):
         return remote(
             dense.at[t, slot], back.at[t, z // 2], send_two.at[t, slot], recv_two.at[t, z // 2],
@@ -324,7 +380,6 @@
             remote(
                 back.at[t, h], back.at[t, h], send_two.at[t, 0], recv_two.at[t, h], (sec, me)
             ).wait_recv()
-    carry_copy.wait()
     for t in range(3):
         def drain(d, carry, t=t):
             one_copy(t, d).wait_send()
@@ -373,11 +428,10 @@
 
 
 def compute_kernel(
-    comp, q, k, v, grad_heads, halo_k, halo_v,
-    answer, local_q, local_k, local_v, carry_grad,
+    comp,
+    answer,
     score, dprob, flip, total_k, total_v,
 ):
-    me = lax.axis_index("seq")
     low = lax.broadcasted_iota(I32, (256, 256), 0)
     col = lax.broadcasted_iota(I32, (256, 256), 1)
     total_k[...] = jnp.zeros_like(total_k)
@@ -401,42 +455,6 @@
         )
         answer[0, rows, :] = (total_k[rows, :] * FACTOR).astype(BF)
         answer[1, rows, :] = total_v[rows, :].astype(BF)
-    first_ok = me > 0
-    for h in range(4):
-        cols = slice((h + 4) * HD, (h + 5) * HD)
-        half = slice(h * HD, (h + 1) * HD)
-
-        def key_rows(n, halo, own):
-            return halo[n * 256 : (n + 1) * 256, half] if n < 2 else own[(n - 2) * 256 : (n - 1) * 256, cols]
-
-        for n in range(4):
-            flip[n] = jnp.transpose(key_rows(n, halo_k, k).astype(F32)).astype(BF)
-        total_k[0:1024, :] = jnp.zeros((1024, HD), F32)
-        total_v[0:1024, :] = jnp.zeros((1024, HD), F32)
-        for blk in range(2):
-            rows = slice(blk * 256, (blk + 1) * 256)
-            masks = [low > col, None, low <= col]
-            for n in range(3):
-                if blk + n < 2:
-                    live = jnp.broadcast_to(first_ok, (256, 256))
-                    masks[n] = live if masks[n] is None else masks[n] & live
-
-            def add(n, dk, dv, blk=blk):
-                spot = slice((blk + n) * 256, (blk + n + 1) * 256)
-                total_k[spot, :] += dk
-                total_v[spot, :] += dv
-
-            local_q[h, rows, :] = attend(
-                score, dprob, q[rows, cols], grad_heads[4 + h, rows, :],
-                lambda n: key_rows(blk + n, halo_k, k),
-                lambda n: key_rows(blk + n, halo_v, v),
-                lambda n: flip[blk + n],
-                masks, add,
-            )
-        carry_grad[0, h] = (total_k[0:512, :] * FACTOR).astype(BF)
-        carry_grad[1, h] = total_v[0:512, :].astype(BF)
-        local_k[h] = total_k[512:1024, :] * FACTOR
-        local_v[h] = total_v[512:1024, :]
 
 
 def finish_kernel(back, carry_in, rank_col, local_q, local_k, local_v, out_q, out_k, out_v):
@@ -450,7 +468,7 @@
         span = slice((h + 4) * HD, (h + 5) * HD)
         out_q[:, span] = local_q[h]
         for t, (out, local) in enumerate(((out_k, local_k), (out_v, local_v))):
-            extra = jnp.where(keep, carry_in[t, h].astype(F32), 0.0)
+            extra = jnp.where(keep, carry_in[h, t].astype(F32), 0.0)
             out[:, span] = (local[h] + extra).astype(BF)
 
 
@@ -489,53 +507,54 @@
     rank_row = jnp.pad(ranks, ((0, 4), (0, 0)))
     rank_col = rank_row.T
     q, k, v = query[0], key[0], value[0]
-    comp, grad_heads, halo_k, halo_v, tab = pl.pallas_call(
+    comp, tab, local_q, local_k, local_v, carry_in = pl.pallas_call(
         forward_kernel,
         out_shape=(
-            SDS((4, 128, 16, HD), BF), SDS((8, 512, HD), BF), SDS((512, 512), BF),
-            SDS((512, 512), BF), SDS((104, 128), I32),
+            SDS((4, 128, 16, HD), BF), SDS((104, 128), I32), SDS((4, 512, HD), BF),
+            SDS((4, 512, HD), F32), SDS((4, 512, HD), F32), SDS((4, 2, 512, HD), BF),
         ),
         in_specs=[VM, VM, VM, HBM, HBM, VM, VM],
-        out_specs=(VM, VM, VM, VM, VM),
+        out_specs=(VM,) * 6,
         scratch_shapes=[
+            pltpu.VMEM((512, 512), BF), pltpu.VMEM((512, 512), BF), pltpu.VMEM((8, 512, HD), BF),
+            pltpu.VMEM((4, 2, 512, HD), BF), pltpu.VMEM((3, 256, 256), F32),
+            pltpu.VMEM((3, 256, 256), F32), pltpu.VMEM((4, HD, 256), BF),
+            pltpu.VMEM((1024, HD), F32), pltpu.VMEM((1024, HD), F32),
             pltpu.VMEM((512, 2048), BF), pltpu.VMEM((1024, 2048), BF),
             pltpu.VMEM((4, 4, 32, 16, HD), BF), *[pltpu.VMEM((4, 32, 16, HD), BF)] * 4,
             pltpu.VMEM((4, 512, 512), BF), pltpu.VMEM((4, 8, 28, 16, HD), BF),
             *[pltpu.VMEM((224, 16, HD), BF)] * 4, pltpu.VMEM((32, 8, 128), I32),
             pltpu.SMEM((104, 128), I32),
             DMA((32,)), DMA, DMA, DMA, DMA, DMA((4, 4)), DMA((4, 4)), DMA((4, 8)), DMA((4, 8)),
-            DMA((2,)), DMA((2,)), DMA,
+            DMA((2,)), DMA((2,)), DMA, DMA((2,)), DMA((2,)),
         ],
         compiler_params=pltpu.CompilerParams(collective_id=0, has_side_effects=True),
         name="exchange_forward",
     )(q, k, v, grad_sent[0], out_weight[0], rank_row, tiles)
-    answer, local_q, local_k, local_v, carry_grad = pl.pallas_call(
+    answer = pl.pallas_call(
         compute_kernel,
-        out_shape=(
-            SDS((3, 2048, HD), BF), SDS((4, 512, HD), BF), SDS((4, 512, HD), F32),
-            SDS((4, 512, HD), F32), SDS((2, 4, 512, HD), BF),
-        ),
-        in_specs=[VM] * 7,
-        out_specs=(VM,) * 5,
+        out_shape=SDS((3, 2048, HD), BF),
+        in_specs=[VM],
+        out_specs=VM,
         scratch_shapes=[
             pltpu.VMEM((8, 256, 256), F32), pltpu.VMEM((8, 256, 256), F32),
             pltpu.VMEM((8, HD, 256), BF), pltpu.VMEM((2048, HD), F32), pltpu.VMEM((2048, HD), F32),
         ],
         name="attention_backward",
-    )(comp.reshape(4, 2048, HD), q, k, v, grad_heads, halo_k, halo_v)
-    back, carry_in = pl.pallas_call(
+    )(comp.reshape(4, 2048, HD))
+    back = pl.pallas_call(
         return_kernel,
-        out_shape=(SDS((3, 4, 32, 16, HD), BF), SDS((2, 4, 512, HD), BF)),
-        in_specs=[VM, VM, SM],
-        out_specs=(VM, VM),
+        out_shape=SDS((3, 4, 32, 16, HD), BF),
+        in_specs=[VM, SM],
+        out_specs=VM,
         scratch_shapes=[
             pltpu.VMEM((3, 8, 28, 16, HD), BF), *[pltpu.VMEM((224, 16, HD), BF)] * 3,
             pltpu.VMEM((3, 4, 32, 16, HD), BF),
-            DMA((3, 8)), DMA((3, 8)), DMA((3, 4)), DMA((3, 4)), DMA, DMA,
+            DMA((3, 8)), DMA((3, 8)), DMA((3, 4)), DMA((3, 4)),
         ],
         compiler_params=pltpu.CompilerParams(collective_id=1, has_side_effects=True),
         name="exchange_return",
-    )(answer.reshape(3, 128, 16, HD), carry_grad, tab)
+    )(answer.reshape(3, 128, 16, HD), tab)
     outs = pl.pallas_call(
         finish_kernel,
         out_shape=(SDS((512, 1024), BF),) * 3,

time: 225 us -> 209 us (0.929); the launches traced: 225 us -> 206 us
  Pallas kernels: 219 us -> 201 us
    pallas_call x2, Pallas kernels: 121 us -> 82.5 us  [the longest x1 70 us: body(): pl.pallas_call(return_kernel, out_shape=SDS((3, 4, 32, 16, HD), BF), in_s...]
    pallas_call x1, Pallas kernels: 92 us -> 112 us  [body(): pl.pallas_call(forward_kernel, out_shape=(SDS((4, 128, 16, HD), BF), SDS(...]
where the time goes in v1:
time: 209 us; the launch traced here: 206 us
  Pallas kernels  201 us (96%)
  local copies, waits for them, and re-layouts  2.35 us (1%)
    pallas_call x1, Pallas kernels, body(): pl.pallas_call(forward_kernel, out_shape=(SDS((4, 128, 16, HD), BF), SDS(...  112 us
    pallas_call x1, Pallas kernels, body(): pl.pallas_call(return_kernel, out_shape=SDS((3, 4, 32, 16, HD), BF), in_s...  70 us
    pallas_call x1, Pallas kernels, body(): pl.pallas_call(compute_kernel, out_shape=SDS((3, 2048, HD), BF), in_specs...  12.5 us
    pallas_call x1, Pallas kernels, body(): pl.pallas_call(finish_kernel, out_shape=(SDS((512, 1024), BF),) * 3, in_s...  6.34 us

profile of v1, /device:TPU:25, one launch (start us, length us, event | category | flops | bytes accessed | tf_op | source)
XLA Modules:
  0.0 206.3 jit_solution(1238452376613967765)
XLA Ops:
  0.7 0.9 convolution_bitcast_fusion
  1.6 0.2 fusion.4
  1.8 0.1 select_reduce_fusion.2
  2.0 0.1 convert_reduce_fusion
  2.1 0.6 stack.16.tiles
  2.7 0.1 copy.23
  2.8 0.2 convert_reduce_fusion.1
  3.0 0.8 select_reduce_fusion
  3.8 0.1 copy.24
  4.0 0.1 copy.27
  4.1 0.7 pad_bitcast_fusion.rank_col
  4.8 0.6 pad.11.clone.rank_row
  5.4 112.0 %exchange_forward.1 = (bf16[4,128,16,128]{3,2,1,0:T(8,128)(2,1)}, s32[104,128]{1,0:T(8,128)}, bf16[4,512,128]{2,1,0:T(8,128)(2,1)}, f32[4,512,128]{2,1,0:T(8,128...) custom-call(bf16[512,1024]{1,0:T(8,128)(2,1)} %bitcast.31, bf16[512,1024]{1,0:T(8,128)(2,1)} %bitcast.32, ...), custom_call_target="tpu_custom_call" | custom-call | tf_op jit(solution)/shard_map/exchange_forward/pallas_call | solution.py:510
  117.4 12.5 %attention_backward.1 = bf16[3,2048,128]{2,1,0:T(8,128)(2,1)} custom-call(bf16[4,2048,128]{2,1,0:T(8,128)(2,1)} %bitcast.29), custom_call_target="tpu_custom_call" | custom-call | tf_op jit(solution)/shard_map/attention_backward/pallas_call | solution.py:534
  129.9 70.0 %exchange_return.1 = bf16[3,4,32,16,128]{4,3,2,1,0:T(8,128)(2,1)} custom-call(bf16[3,128,16,128]{3,2,1,0:T(8,128)(2,1)} %bitcast.26, s32[104,128]{1,0:T(8,128)} %get-tuple-element.13.table), custom_call_target="tpu_custom_call" | custom-call | tf_op jit(solution)/shard_map/exchange_return/pallas_call | solution.py:545
  199.9 6.3 %finish.1 = (bf16[512,1024]{1,0:T(8,128)(2,1)}, bf16[512,1024]{1,0:T(8,128)(2,1)}, bf16[512,1024]{1,0:T(8,128)(2,1)}) custom-call(bf16[3,4,512,128]{3,2,1,0:T(8,128)(2,1)} %bitcast.27, bf16[4,2,512,128]{3,2,1,0:T(8,128)(2,1)} %get-tuple-element.14.carry_in, s32[512,8]{1,0:T(8,128)} %pad_bitcast_fusion.rank_col, ...), custom_call_target="tpu_custom_call" | custom-call | tf_op jit(solution)/shard_map/finish/pallas_call | solution.py:558
  (10 shorter events, 0.1 us)
